TPU v7x, 512 devices: a whole 4x4x16 slice. The times are simulated.
512 devices in a mesh: gx: 8 (over y, z_hi), gy: 8 (over x, core), gz: 8 (over z_lo).
Axes of the slice: x: 4, y: 4, z: 16 (z_hi: 2, z_lo: 8; z = z_hi * 8 + z_lo), core: 2. Of those that a mesh axis runs over, the one named last changes fastest.
Arguments:
- gradients: bfloat16 [524288, 128], P(('gx', 'gy', 'gz')), may hold values from -4 to 4
- row_ids: int32 [524288], P(('gx', 'gy', 'gz')), may hold values from 0 to 131071, as said below
- hot_ids: int32 [1024], replicated, may hold values from 0 to 131071, as said below
- embedding: float32 [131072, 128], P(('gx', 'gy', 'gz')), may hold values from -4 to 4
- moments: float32 [131072, 128], P(('gx', 'gy', 'gz')), may hold values from 0.5 to 4
- hot_table: float32 [1024, 128], replicated, may hold values from -4 to 4
- hot_moments: float32 [1024, 128], replicated, may hold values from 4 to 64
Outputs:
- new_table: float32 [131072, 128], P(('gx', 'gy', 'gz'))
- new_moments: float32 [131072, 128], P(('gx', 'gy', 'gz'))
- new_hot_table: float32 [1024, 128], replicated
- new_hot_moments: float32 [1024, 128], replicated
Inputs may be any that keep to these rules, and one draw needn't show every extreme that they name: `row_ids`: for each device, its row ids that are not in hot_ids fall on at most 4 distinct rows of any one owner's range of 256 rows (owner = id // 256, devices in the order gx, gy, gz); in every draw some owner gets exactly 4 such distinct ids from every device. `hot_ids`: 1024 distinct ids.
All inputs are finite; a program needn't handle non-finite values.
Results may differ from a plain program's by a relative error of at most 0.0003.
Values sent between devices are 32-bit elements; how exact they have to be, the bound alone decides.
A program may use at most 64 MiB of HBM per device.

v0:
```python
import jax
import jax.numpy as jnp
from jax import lax
from jax.sharding import Mesh
from jax.sharding import PartitionSpec as P

CAP = 4
GX = ("gx_0", "gx_1")
GY = ("gy_0", "gy_1")
GX_GY_GZ = ("gx_0", "gx_1", "gy_0", "gy_1", "gz")
GX_GY = ("gx_0", "gx_1", "gy_0", "gy_1")


def padded_to(lines, devices):
    spare = -len(lines) % devices
    return jnp.pad(lines, [(0, spare)] + [(0, 0)] * (lines.ndim - 1))


def own_block(tiles, axes, turns):
    inside = tiles.shape[1:]
    tiles = tiles.reshape(*(lax.axis_size(a) for a in axes), *inside)
    tiles = jnp.moveaxis(tiles, turns, range(len(axes))).reshape(-1, *inside)
    for k in turns:
        tiles = lax.psum_scatter(tiles, axes[k], scatter_dimension=0, tiled=True)
    return tiles[0]


def all_blocks(x, axes, turns):
    tiles = x[None]
    for k in turns:
        tiles = lax.all_gather(tiles, axes[k], axis=0, tiled=True)
    block = [lax.axis_size(axes[k]) for k in reversed(turns)]
    tiles = tiles.reshape(*block, *x.shape)
    turned = sorted(range(len(turns)), key=lambda place: turns[len(turns) - 1 - place])
    return tiles.transpose(*turned, *range(len(turns), tiles.ndim)).reshape(-1, *x.shape)


def sum_at_once(x, axes):
    devices, count = (lax.axis_size(axes), len(axes))
    lines = x.reshape(-1, *x.shape[1:][-1:])
    tiles = padded_to(lines, devices * count).reshape(count, devices, -1, *lines.shape[1:])
    finished = []
    for initial in range(count):
        turns = [(initial + k) % count for k in range(count)]
        own = own_block(tiles[initial], axes, turns)
        finished.append(all_blocks(own, axes, turns[::-1]).reshape(-1, *lines.shape[1:]))
    return jnp.concatenate(finished)[: len(lines)].reshape(x.shape)


def cut_along(x, dim, devices):
    before, after = (x.shape[:dim], x.shape[dim + 1 :])
    return jnp.moveaxis(x.reshape(*before, devices, -1, *after), dim, 0)


def in_order(tiles, dim):
    tiles = jnp.moveaxis(tiles, 0, dim)
    dims = tiles.shape
    return tiles.reshape(*dims[:dim], dims[dim] * dims[dim + 1], *dims[dim + 2 :])


def joined_exchange(x, axis, axes, splits, concats):
    sizes = [lax.axis_size(a) for a in axes]
    tiles = cut_along(x, splits[0], sizes[0])
    tiles = jnp.moveaxis(cut_along(tiles, splits[1] + 1, sizes[1]), 0, 1)
    inside = tiles.shape[2:]
    tiles = tiles.reshape(-1, *inside)
    tiles = lax.all_to_all(tiles, axis, split_axis=0, concat_axis=0, tiled=True)
    tiles = in_order(tiles.reshape(*sizes, *inside), concats[0] + 1)
    return in_order(tiles, concats[1])


def adagrad(weights, moments, gradient):
    updated = moments + gradient * gradient
    return (weights - 0.5 * gradient / (jnp.sqrt(updated) + 1e-06), updated)


def body(gradients, row_ids, hot_ids, embedding, moments, hot_table, hot_moments):
    tokens = row_ids.shape[0]
    rows_local = embedding.shape[0]
    features = gradients.shape[1]
    plane_size = lax.axis_size(GX) * lax.axis_size(GY)
    depth_size = lax.axis_size("gz")
    devices = plane_size * depth_size
    capacity = CAP
    buckets = devices * capacity
    block_rows = min(512, tokens)
    block_count = tokens // block_rows
    group_rows = min(512, buckets)
    matched = row_ids[:, None] == hot_ids[None, :]
    is_hot = jnp.any(matched, axis=1)
    hot_local = jnp.einsum(
        "th,te->he", matched.astype(jnp.bfloat16), gradients, preferred_element_type=jnp.float32
    )
    hot_grad = sum_at_once(hot_local, GX_GY_GZ)
    new_hot_table, new_hot_moments = adagrad(hot_table, hot_moments, hot_grad)
    owners = row_ids // rows_local
    local_rows = row_ids % rows_local
    is_cold = jnp.logical_not(is_hot)
    position = jnp.arange(tokens, dtype=jnp.int32)
    id_blocks = row_ids.reshape(block_count, block_rows)
    pos_blocks = position.reshape(block_count, block_rows)
    owner_blocks = owners.reshape(block_count, block_rows)

    def earlier(operands):
        block_ids, block_pos = operands
        repeated = (block_ids[:, None] == row_ids[None, :]) & (
            position[None, :] < block_pos[:, None]
        )
        return jnp.logical_not(jnp.any(repeated, axis=1))

    leading = lax.map(earlier, (id_blocks, pos_blocks)).reshape(tokens) & is_cold

    def ranking(operands):
        block_ids, block_owner = operands
        smaller = (
            (owners[None, :] == block_owner[:, None])
            & (row_ids[None, :] < block_ids[:, None])
            & leading[None, :]
        )
        return jnp.sum(smaller.astype(jnp.int32), axis=1)

    slot_index = lax.map(ranking, (id_blocks, owner_blocks)).reshape(tokens)
    bucket = jnp.where(is_cold, owners * capacity + slot_index, buckets)

    def assemble(targets):
        onehot = (targets[:, None] == bucket[None, :]).astype(jnp.bfloat16)
        return jnp.dot(onehot, gradients, preferred_element_type=jnp.float32)

    target_groups = jnp.arange(buckets, dtype=jnp.int32).reshape(buckets // group_rows, group_rows)
    outgoing = lax.map(assemble, target_groups).reshape(plane_size, depth_size, capacity, features)
    landing = jnp.where(leading, bucket, buckets)
    labels = (
        jnp.zeros((buckets,), jnp.float32)
        .at[landing]
        .set(local_rows.astype(jnp.float32), mode="drop")
    )
    labels = labels.reshape(plane_size, depth_size, capacity)
    incoming, arrived = (
        joined_exchange(outgoing, GX_GY_GZ, (GX_GY, "gz"), (0, 1), (0, 1)),
        joined_exchange(labels, GX_GY_GZ, (GX_GY, "gz"), (0, 1), (0, 1)),
    )
    gathered = incoming.reshape(buckets, features)
    where_rows = arrived.reshape(buckets).astype(jnp.int32)
    gradient = jnp.zeros((rows_local, features), jnp.float32).at[where_rows].add(gathered)
    new_table, new_moments = adagrad(embedding, moments, gradient)
    return (new_table, new_moments, new_hot_table, new_hot_moments)


def solution(mesh):
    torus = Mesh(
        mesh.devices.reshape(4, 2, 4, 2, mesh.shape["gz"]), ("gx_0", "gx_1", "gy_0", "gy_1", "gz")
    )
    placed = (P(GX_GY_GZ, None), P(GX_GY_GZ), P(), P(GX_GY_GZ, None), P(GX_GY_GZ, None), P(), P())
    return jax.shard_map(
        body,
        mesh=torus,
        in_specs=placed,
        out_specs=(P(GX_GY_GZ, None), P(GX_GY_GZ, None), P(), P()),
        check_vma=False,
    )
```

profile of v0, /device:TPU:1, one launch (start us, length us, event | category | flops | bytes accessed | tf_op | source)
XLA Modules:
  0.0 482.5 jit_solution(18197822455225809726)
XLA Ops:
  7.2 0.7 reshape.105
  7.9 0.7 add_select_fusion.1
  8.6 2.9 while.33
  8.6 1.4 fusion.36
  10.1 1.4 fusion.36
  11.5 1.4 compare_reduce_fusion
  12.9 2.7 while.31
  12.9 1.3 convert_reduce_fusion.2
  14.3 1.3 convert_reduce_fusion.2
  15.7 0.7 compare_select_fusion.1
  16.4 4.3 scatter_custom_fusion
  20.7 1.0 reshape_transpose_transpose_reshape_reshape_reshape.6
  21.6 24.3 %all-to-all-start = ((f32[512,1,1,4]{3,2,1,0:T(1,128)}), f32[512,1,1,4]{3,2,1,0:T(1,128)S(1)}, u32[]{:S(2)}, u32[]{:S(2)}) async-start(f32[512,1,1,4]{3,2,1,0:T(1,128)} %bitcast.5), calls=%async_computation | async-start | bytes 524288 | tf_op jit(solution)/shard_map/all_to_all | solution.py:67
  46.0 4.8 %while.32 = (s32[]{:T(128)}, f32[4,512,128]{2,1,0:T(8,128)}, s32[4,512]{1,0:T(4,128)S(1)}, s32[1024]{0:T(1024)S(1)}, bf16[1024,128]{1,0:T(8,128)(2,1)S(1)}, /*index=5*/s32[]{:T(128)}) while((s32[]{:T(128)}, f32[4,512,128]{2,1,0:T(8,128)}, s32[4,512]{1,0:T(4,128)S(1)}, s32[1024]{0:T(1024)S(1)}, bf16[1024,128]{1,0:T(8,128)(2,1)S(1)}, ...), condition=%wide.region_9.10_spmd, body=%wide.region_8.9_spmd.sunk | while | flops 134742016 | bytes 535113 | solution.py:130
  46.0 1.2 fusion.35
  47.2 1.2 fusion.35
  48.4 1.2 fusion.35
  49.6 1.2 fusion.35
  50.8 19.8 %all-to-all-done = f32[512,1,1,4]{3,2,1,0:T(1,128)S(1)} async-done(((f32[512,1,1,4]{3,2,1,0:T(1,128)}), f32[512,1,1,4]{3,2,1,0:T(1,128)S(1)}, u32[]{:S(2)}, u32[]{:S(2)}) %all-to-all-start) | async-done | bytes 8224 | tf_op jit(solution)/shard_map/all_to_all | solution.py:67
  70.6 9.3 %all-to-all-start.1 = ((f32[512,1,1,4,128]{4,3,2,1,0:T(4,128)}), f32[512,1,1,4,128]{4,3,2,1,0:T(4,128)S(1)}, u32[]{:S(2)}, u32[]{:S(2)}) async-start(f32[512,1,1,4,128]{4,3,2,1,0:T(4,128)} %bitcast.11), calls=%async_computation.1 | async-start | bytes 2097152 | tf_op jit(solution)/shard_map/all_to_all | solution.py:67
  79.9 0.0 reduce-scatter.11.cloned.1.call-start
  80.0 1.4 fusion.14
  81.4 0.7 slice_bitcast_fusion
  82.1 0.0 reduce-scatter.11.cloned.1.call-update
  82.2 0.0 reduce-scatter.13.cloned.1.call-start
  82.2 31.6 %reduce-scatter.11.cloned.1.call-done = f32[128,1,128]{2,0,1:T(8,128)} async-done(((f32[512,1,128]{2,0,1:T(8,128)}), f32[128,1,128]{2,0,1:T(8,128)}) %reduce-scatter.11.cloned.1.call-update) | async-done | bytes 65552 | tf_op jit(solution)/shard_map/reduce_scatter | solution.py:24
  113.8 0.0 reduce-scatter.13.cloned.1.call-update
  113.9 0.0 reduce-scatter.17.cloned.1.call-start
  113.9 0.9 copy.28
  114.8 0.0 reduce-scatter.17.cloned.1.call-update
  114.8 0.0 reduce-scatter.15.cloned.1.call-start
  114.8 34.3 %reduce-scatter.13.cloned.1.call-done = f32[64,1,128]{2,0,1:T(8,128)} async-done(((f32[128,1,128]{2,0,1:T(8,128)}), f32[64,1,128]{2,0,1:T(8,128)}) %reduce-scatter.13.cloned.1.call-update) | async-done | bytes 32784 | tf_op jit(solution)/shard_map/reduce_scatter | solution.py:24
  149.2 0.0 reduce-scatter.15.cloned.1.call-update
  149.2 0.0 reduce-scatter.19.cloned.1.call-start
  149.2 1.3 dynamic-slice
  150.5 1.3 dynamic-slice.2
  151.8 1.3 dynamic-slice.6
  154.3 0.2 convert_element_type.38
  154.6 0.2 convert_element_type.37
  154.7 29.2 %reduce-scatter.17.cloned.1.call-done = f32[256,1,128]{2,0,1:T(8,128)} async-done(((f32[512,1,128]{2,0,1:T(8,128)}), f32[256,1,128]{2,0,1:T(8,128)}) %reduce-scatter.17.cloned.1.call-update) | async-done | bytes 131088 | tf_op jit(solution)/shard_map/reduce_scatter | solution.py:24
  183.9 0.0 reduce-scatter.19.cloned.1.call-update
  183.9 0.0 reduce-scatter.21.cloned.1.call-start
  184.0 19.9 %reduce-scatter.15.cloned.1.call-done = f32[16,1,128]{2,0,1:T(8,128)} async-done(((f32[64,1,128]{2,0,1:T(8,128)}), f32[16,1,128]{2,0,1:T(8,128)}) %reduce-scatter.15.cloned.1.call-update) | async-done | bytes 8208 | tf_op jit(solution)/shard_map/reduce_scatter | solution.py:24
  203.9 5.2 %all-reduce = f32[16,1,128]{2,0,1:T(8,128)S(1)} all-reduce(f32[16,1,128]{2,0,1:T(8,128)} %reduce-scatter.15.cloned.1.call-done), channel_id=5, replica_groups=mesh['gx_0'=4,'gx_1'=2,'gy_0'=4,'gy_1'=2,'gz'=8] {'gy_1'}, use_global_device_ids=true, to_apply=%region_14.15.clone | all-reduce | flops 2048 | bytes 16384
  209.1 25.6 %reduce-scatter.19.cloned.1.call-done = f32[64,1,128]{2,0,1:T(8,128)} async-done(((f32[256,1,128]{2,0,1:T(8,128)}), f32[64,1,128]{2,0,1:T(8,128)}) %reduce-scatter.19.cloned.1.call-update) | async-done | bytes 32784 | tf_op jit(solution)/shard_map/reduce_scatter | solution.py:24
  234.7 0.0 reduce-scatter.21.cloned.1.call-update
  234.7 24.1 %reduce-scatter.21.cloned.1.call-done = f32[32,1,128]{2,0,1:T(8,128)} async-done(((f32[64,1,128]{2,0,1:T(8,128)}), f32[32,1,128]{2,0,1:T(8,128)}) %reduce-scatter.21.cloned.1.call-update) | async-done | bytes 16400 | tf_op jit(solution)/shard_map/reduce_scatter | solution.py:24
  258.9 49.1 %all-reduce.4 = (f32[32,1,128]{2,0,1:T(8,128)S(1)}, f32[8,1,128]{2,0,1:T(8,128)S(1)}) all-reduce(f32[32,1,128]{2,0,1:T(8,128)} %reduce-scatter.21.cloned.1.call-done, f32[8,1,128]{2,0,1:T(8,128)S(1)} %constant_dynamic-slice_fusion.8), channel_id=10, replica_groups=mesh['gx_0'=4,'gx_1'=2,'gy_0'=4,'gy_1'=2,'gz'=8] {'gz'}, use_global_device_ids=true, to_apply=%region_19.20.clone | all-reduce | flops 5120 | bytes 40960
  308.0 8.7 %all-reduce.3 = f32[4,1,128]{2,0,1:T(4,128)S(1)} all-reduce(f32[4,1,128]{2,0,1:T(4,128)S(1)} %constant_dynamic-slice_fusion.6), channel_id=11, replica_groups=mesh['gx_0'=4,'gx_1'=2,'gy_0'=4,'gy_1'=2,'gz'=8] {'gx_0'}, use_global_device_ids=true, to_apply=%region_20.21.clone | all-reduce | flops 512 | bytes 4096
  316.7 0.6 fusion.26
  317.4 5.2 %all_gather.50 = f32[4,1,128]{2,1,0:T(1,128)S(1)} all-gather(f32[1,1,128]{2,1,0:T(1,128)S(1)} %fusion.26), channel_id=1, replica_groups=mesh['gx_0'=4,'gx_1'=2,'gy_0'=4,'gy_1'=2,'gz'=8] {'gx_0'}, dimensions={0}, use_global_device_ids=true | all-gather | bytes 2560 | tf_op jit(solution)/shard_map/all_gather | solution.py:31
  322.6 37.4 %all_gather.51 = f32[32,1,128]{2,1,0:T(1,128)S(1)} all-gather(f32[4,1,128]{2,1,0:T(1,128)S(1)} %all_gather.50), channel_id=1, replica_groups=mesh['gx_0'=4,'gx_1'=2,'gy_0'=4,'gy_1'=2,'gz'=8] {'gz'}, dimensions={0}, use_global_device_ids=true | all-gather | bytes 18432 | tf_op jit(solution)/shard_map/all_gather | solution.py:31
  360.0 17.8 %all_gather.52 = f32[64,1,128]{2,0,1:T(8,128)S(1)} all-gather(f32[32,1,128]{2,0,1:T(8,128)S(1)} %bitcast.87), channel_id=1, replica_groups=mesh['gx_0'=4,'gx_1'=2,'gy_0'=4,'gy_1'=2,'gz'=8] {'gy_1'}, dimensions={0}, use_global_device_ids=true | all-gather | bytes 49152 | tf_op jit(solution)/shard_map/all_gather | solution.py:31
  377.8 9.7 %all_gather.53 = f32[256,1,128]{2,0,1:T(8,128)S(1)} all-gather(f32[64,1,128]{2,0,1:T(8,128)S(1)} %all_gather.52), channel_id=1, replica_groups=mesh['gx_0'=4,'gx_1'=2,'gy_0'=4,'gy_1'=2,'gz'=8] {'gy_0'}, dimensions={0}, use_global_device_ids=true | all-gather | bytes 163840 | tf_op jit(solution)/shard_map/all_gather | solution.py:31
  387.5 14.4 %all_gather.54 = f32[512,1,128]{2,0,1:T(8,128)S(1)} all-gather(f32[256,1,128]{2,0,1:T(8,128)S(1)} %all_gather.53), channel_id=1, replica_groups=mesh['gx_0'=4,'gx_1'=2,'gy_0'=4,'gy_1'=2,'gz'=8] {'gx_1'}, dimensions={0}, use_global_device_ids=true | all-gather | bytes 393216 | tf_op jit(solution)/shard_map/all_gather | solution.py:31
  402.0 0.7 fusion.25
  402.6 20.8 %all_gather.20 = f32[8,1,128]{2,1,0:T(1,128)S(1)} all-gather(f32[1,1,128]{2,1,0:T(1,128)S(1)} %fusion.25), channel_id=1, replica_groups=mesh['gx_0'=4,'gx_1'=2,'gy_0'=4,'gy_1'=2,'gz'=8] {'gz'}, dimensions={0}, use_global_device_ids=true | all-gather | bytes 4608 | tf_op jit(solution)/shard_map/all_gather | solution.py:31
  423.4 7.7 %all_gather.21 = f32[16,1,128]{2,0,1:T(8,128)S(1)} all-gather(f32[8,1,128]{2,0,1:T(8,128)S(1)} %bitcast.89), channel_id=1, replica_groups=mesh['gx_0'=4,'gx_1'=2,'gy_0'=4,'gy_1'=2,'gz'=8] {'gy_1'}, dimensions={0}, use_global_device_ids=true | all-gather | bytes 12288 | tf_op jit(solution)/shard_map/all_gather | solution.py:31
  431.1 9.0 %all_gather.22 = f32[64,1,128]{2,0,1:T(8,128)S(1)} all-gather(f32[16,1,128]{2,0,1:T(8,128)S(1)} %all_gather.21), channel_id=1, replica_groups=mesh['gx_0'=4,'gx_1'=2,'gy_0'=4,'gy_1'=2,'gz'=8] {'gy_0'}, dimensions={0}, use_global_device_ids=true | all-gather | bytes 40960 | tf_op jit(solution)/shard_map/all_gather | solution.py:31
  440.1 12.1 %all_gather.23 = f32[128,1,128]{2,0,1:T(8,128)S(1)} all-gather(f32[64,1,128]{2,0,1:T(8,128)S(1)} %all_gather.22), channel_id=1, replica_groups=mesh['gx_0'=4,'gx_1'=2,'gy_0'=4,'gy_1'=2,'gz'=8] {'gx_1'}, dimensions={0}, use_global_device_ids=true | all-gather | bytes 98304 | tf_op jit(solution)/shard_map/all_gather | solution.py:31
  452.2 9.9 %all_gather.24 = f32[512,1,128]{2,0,1:T(8,128)S(1)} all-gather(f32[128,1,128]{2,0,1:T(8,128)S(1)} %all_gather.23), channel_id=1, replica_groups=mesh['gx_0'=4,'gx_1'=2,'gy_0'=4,'gy_1'=2,'gz'=8] {'gx_0'}, dimensions={0}, use_global_device_ids=true | all-gather | bytes 327680 | tf_op jit(solution)/shard_map/all_gather | solution.py:31
  462.1 1.2 divide_subtract_fusion
  463.3 11.5 %scatter_custom_fusion.1 = f32[256,128]{1,0:T(8,128)S(1)} fusion(s32[2048]{0:T(1024)S(1)} %bitcast.91, f32[2048,128]{1,0:T(8,128)S(1)} %bitcast.77, f32[]{:T(128)} %constant.72.clone.1), kind=kCustom, calls=%fused_computation.29 | custom fusion | flops 262144 | bytes 131076 | tf_op jit(solution)/shard_map/scatter-add | solution.py:144
  474.9 0.8 divide_subtract_fusion.1
  (44 shorter events, 0.4 us)
Async XLA Ops:
  7.2 38.8 %copy-start.6 = (bf16[1024,128]{1,0:T(8,128)(2,1)S(1)}, bf16[1024,128]{1,0:T(8,128)(2,1)}, u32[]{:S(2)}) copy-start(bf16[1024,128]{1,0:T(8,128)(2,1)} %param.13) | copy-start | bytes 786436
  21.6 48.9 %all-to-all-start = ((f32[512,1,1,4]{3,2,1,0:T(1,128)}), f32[512,1,1,4]{3,2,1,0:T(1,128)S(1)}, u32[]{:S(2)}, u32[]{:S(2)}) async-start(f32[512,1,1,4]{3,2,1,0:T(1,128)} %bitcast.5), calls=%async_computation | async-start | bytes 524288 | tf_op jit(solution)/shard_map/all_to_all | solution.py:67
  70.6 9.4 %copy-start = (s32[1024]{0:T(1024)S(1)}, s32[1024]{0:T(1024)}, u32[]{:S(2)}) copy-start(s32[1024]{0:T(1024)} %get-tuple-element.356) | copy-start | bytes 12292
  70.6 9.4 %copy-start.5 = (s32[1024]{0:T(1024)S(1)}, s32[1024]{0:T(1024)}, u32[]{:S(2)}) copy-start(s32[1024]{0:T(1024)} %param.15) | copy-start | bytes 12292
  70.6 392.8 %all-to-all-start.1 = ((f32[512,1,1,4,128]{4,3,2,1,0:T(4,128)}), f32[512,1,1,4,128]{4,3,2,1,0:T(4,128)S(1)}, u32[]{:S(2)}, u32[]{:S(2)}) async-start(f32[512,1,1,4,128]{4,3,2,1,0:T(4,128)} %bitcast.11), calls=%async_computation.1 | async-start | bytes 2097152 | tf_op jit(solution)/shard_map/all_to_all | solution.py:67
  79.9 33.9 %reduce-scatter.11.cloned.1.call-start = ((), (), s32[]{:S(2)}) async-start(), calls=%async_computation.8 | async-start | bytes 327680 | tf_op jit(solution)/shard_map/reduce_scatter | solution.py:24
  82.2 67.0 %reduce-scatter.13.cloned.1.call-start = ((), (), s32[]{:S(2)}) async-start(), calls=%async_computation.9 | async-start | bytes 98304 | tf_op jit(solution)/shard_map/reduce_scatter | solution.py:24
  113.9 70.0 %reduce-scatter.17.cloned.1.call-start = ((), (), s32[]{:S(2)}) async-start(), calls=%async_computation.11 | async-start | bytes 393216 | tf_op jit(solution)/shard_map/reduce_scatter | solution.py:24
  114.8 89.1 %reduce-scatter.15.cloned.1.call-start = ((), (), s32[]{:S(2)}) async-start(), calls=%async_computation.10 | async-start | bytes 40960 | tf_op jit(solution)/shard_map/reduce_scatter | solution.py:24
  149.2 85.5 %reduce-scatter.19.cloned.1.call-start = ((), (), s32[]{:S(2)}) async-start(), calls=%async_computation.12 | async-start | bytes 163840 | tf_op jit(solution)/shard_map/reduce_scatter | solution.py:24
  154.5 307.6 %copy-start.1 = (f32[1024,128]{1,0:T(8,128)S(1)}, f32[1024,128]{1,0:T(8,128)}, u32[]{:S(2)}) copy-start(f32[1024,128]{1,0:T(8,128)} %param.18) | copy-start | bytes 1572868
  154.5 307.6 %copy-start.2 = (f32[1024,128]{1,0:T(8,128)S(1)}, f32[1024,128]{1,0:T(8,128)}, u32[]{:S(2)}) copy-start(f32[1024,128]{1,0:T(8,128)} %param.19) | copy-start | bytes 1572868
  183.9 74.9 %reduce-scatter.21.cloned.1.call-start = ((), (), s32[]{:S(2)}) async-start(), calls=%async_computation.13 | async-start | bytes 49152 | tf_op jit(solution)/shard_map/reduce_scatter | solution.py:24
  462.1 12.7 %copy-start.3 = (f32[256,128]{1,0:T(8,128)S(1)}, f32[256,128]{1,0:T(8,128)}, u32[]{:S(2)}) copy-start(f32[256,128]{1,0:T(8,128)} %param.16) | copy-start | bytes 393220
  462.1 12.7 %copy-start.4 = (f32[256,128]{1,0:T(8,128)S(1)}, f32[256,128]{1,0:T(8,128)}, u32[]{:S(2)}) copy-start(f32[256,128]{1,0:T(8,128)} %param.17) | copy-start | bytes 393220
Sparse Core Ops, SparseCore 0:
  84.1 29.6 reduce-scatter.10
  116.6 32.5 reduce-scatter.12
  152.5 31.3 reduce-scatter.16
  186.5 17.2 reduce-scatter.14
  206.5 28.1 reduce-scatter.18
  237.3 21.5 reduce-scatter.20
where the time goes:
time: 489 us; the launch traced here: 482 us
  blocking collectives  207 us (42%)
  waiting for transfers between devices  185 us (38%)
  starting transfers between devices  33.9 us (7%)
  other arithmetic  21.7 us (4%)
  between operations  15.6 us (3%)
  local copies, waits for them, and re-layouts  13.2 us (3%)
  matrix products  6.2 us (1%)
    reduce_scatter x6, waiting for transfers between devices, own_block(): tiles = lax.psum_scatter(tiles, axes[k], scatter_dimension=0, tiled=True)  165 us
    all_gather x10, blocking collectives, all_blocks(): tiles = lax.all_gather(tiles, axes[k], axis=0, tiled=True)  144 us
    unnamed x3, blocking collectives  63 us
    all_to_all x2, starting transfers between devices, joined_exchange(): tiles = lax.all_to_all(tiles, axis, split_axis=0, concat_axis=0, tiled=True)  33.6 us
    all_to_all x2, waiting for transfers between devices, joined_exchange(): tiles = lax.all_to_all(tiles, axis, split_axis=0, concat_axis=0, tiled=True)  19.8 us
    scatter-add x1, other arithmetic, body(): jnp.zeros((rows_local, features), jnp.float32).at[where_rows].add(gathered)  11.5 us
  transfers between devices with their start and end apart: 8, of which 7 were waited for; matrix products, arithmetic and copies ran while one was open for 3% of the time, Pallas kernels for 0%

commit v1 on v0

v1 whole, which is shorter than its diff:
```python
import functools

import jax
import jax.numpy as jnp
from jax import lax
from jax.experimental import pallas as pl
from jax.experimental.pallas import tpu as pltpu
from jax.sharding import Mesh
from jax.sharding import PartitionSpec as P

AXES = ("gx_0", "gx_1", "gy_0", "gy_1", "gz")
CAP = 4
ROWS = 256
BIG = 1.0e9
SUB = 4
MESH = pl.DeviceIdType.MESH
F32, BF16, I32 = jnp.float32, jnp.bfloat16, jnp.int32


def kernel(
    sizes, ids_ref, hot_ref, grad_ref, cold_ref, hotg_ref,
    mc, sb, rb, lt, lr, labs, dp, fw, bw, hs, hr, hp, hz, hq, hg, ho,
    ssem, rsem, lsem, zsend, fsem, bsem, hsem, sent,
):
    ny, nzh, nx, nc, nzl = sizes
    np_, nz = ny * nx * nc, nzh * nzl
    half = nz // 2
    tiles = ids_ref.shape[0]
    hot_rows = hs.shape[1]
    classes = hot_rows // 8
    y, zh, x, c, zl = (lax.axis_index(a) for a in AXES)
    me_p = (y * nx + x) * nc + c
    me_z = zh * nzl + zl

    def plane(p):
        return (p // (nx * nc), zh, (p // nc) % nx, p % nc, zl)

    def column(z):
        return (y, z // nzl, x, c, z % nzl)

    def mate(k):
        return lax.rem(me_p + k, np_)

    def above(k):
        return lax.rem(me_z + k, nz)

    def remote(src, dst, send, recv, device):
        return pltpu.make_async_remote_copy(
            src_ref=src, dst_ref=dst, send_sem=send, recv_sem=recv,
            device_id=device, device_id_type=MESH,
        )

    def whole(ref, sem):
        pltpu.make_async_copy(ref, ref, sem).wait()

    barrier = pltpu.get_barrier_semaphore()

    @pl.loop(1, np_)
    def _(k):
        pl.semaphore_signal(barrier, inc=1, device_id=plane(mate(k)), device_id_type=MESH)

    @pl.loop(1, nz)
    def _(k):
        pl.semaphore_signal(barrier, inc=1, device_id=column(above(k)), device_id_type=MESH)

    ids = [ids_ref[k : k + 1, :] for k in range(tiles)]
    idf = [v.astype(F32) for v in ids]
    grads = grad_ref[...]

    def match(i, found):
        row = hot_ref[pl.ds(i, 1), :].astype(F32)
        column_of = jnp.transpose(jnp.broadcast_to(row, (128, 128)))
        hits = [jnp.where(column_of == idf[k], 1.0, 0.0) for k in range(tiles)]
        sums = jnp.dot(
            jnp.concatenate(hits, axis=1).astype(BF16), grads, preferred_element_type=F32
        )
        parts = 128 // hot_rows
        hs[pl.ds(i * parts, parts)] = sums.reshape(parts, hot_rows, 128)
        return tuple(f + jnp.sum(h.reshape(16, 8, 128), axis=0) for f, h in zip(found, hits))

    none = tuple(jnp.zeros((8, 128), F32) for _ in range(tiles))
    found = lax.fori_loop(0, hot_ref.shape[0], match, none)

    owner = []
    for k in range(tiles):
        o = ids[k] // ROWS
        oz = (o // (nx * nc * nzl)) % nzh * nzl + o % nzl
        op = (o // (nx * nc * nzl * nzh) * nx + o // (nc * nzl) % nx) * nc + o // nzl % nc
        rel = (oz - me_z + nz) % nz
        step = jnp.where(rel == 0, 0, jnp.where(rel <= half, half - rel, rel - half))
        side = jnp.where((rel > half) | (rel == 0), 1, 0)
        place = (step * np_ + op) * 2 + side
        hot = jnp.sum(found[k], axis=0, keepdims=True) > 0.0
        owner.append(jnp.where(hot, -1, place))
    span = min(32, np_ * nz)

    def pick(b, carry):
        mine = lax.broadcasted_iota(I32, (span, 128), 0) + b * span
        left = [jnp.where(owner[k] == mine, idf[k], BIG) for k in range(tiles)]
        for j in range(CAP):
            low = left[0]
            for v in left[1:]:
                low = jnp.minimum(low, v)
            low = jnp.min(low, axis=1, keepdims=True)
            mc[pl.ds(b * span * CAP + j, span, stride=CAP), :] = jnp.broadcast_to(low, (span, 128))
            if j < CAP - 1:
                left = [jnp.where(v > low, v, BIG) for v in left]
        return carry

    lax.fori_loop(0, np_ * nz // span, pick, 0)

    group = np_ * 8
    lane = lax.broadcasted_iota(I32, (group, 128), 1)

    def label(s, total):
        low = mc[pl.ds(pl.multiple_of(s * group, group), group), :]
        value = jnp.where(low < BIG, (low.astype(I32) % ROWS + 1).astype(F32), 0.0)
        return jnp.where(lane == s, value, total)

    lt[...] = lax.fori_loop(0, half, label, jnp.zeros((group, 128), F32)).reshape(np_, 8, 128)

    pl.semaphore_wait(barrier, np_ - 1 + nz - 1)

    @pl.loop(1, np_)
    def _(k):
        p = mate(k)
        remote(lt.at[p], lr.at[me_p], sent.at[0], lsem, plane(p)).start()

    pltpu.make_async_copy(lt.at[me_p], lr.at[me_p], lsem).start()

    @pl.loop(0, half)
    def _(s):
        low = mc[pl.ds(pl.multiple_of(s * group, group), group), :]
        hits = [jnp.where(low == idf[k], 1.0, 0.0).astype(BF16) for k in range(tiles)]
        sums = jnp.dot(jnp.concatenate(hits, axis=1), grads, preferred_element_type=F32)
        sb[s] = sums.reshape(np_, 8, 128)

        @pl.loop(1, np_)
        def _(k):
            p = mate(k)
            remote(sb.at[s, p], rb.at[s, me_p], ssem.at[s], rsem.at[s], plane(p)).start()

        pltpu.make_async_copy(sb.at[s, me_p], rb.at[s, me_p], rsem.at[s]).start()

        @pl.when(s == 0)
        def _():
            @pl.loop(1, np_)
            def _(k):
                p = mate(k)
                remote(hs.at[p], hr.at[me_p], sent.at[1], hsem.at[0], plane(p)).start()

            pltpu.make_async_copy(hs.at[me_p], hr.at[me_p], hsem.at[0]).start()

    whole(lr, lsem)
    eye = lax.broadcasted_iota(I32, (8, 128), 0) == lax.broadcasted_iota(I32, (8, 128), 1)
    eye = jnp.where(eye, 1.0, 0.0).astype(BF16)
    rows = lax.dot_general(
        eye, lr[...].reshape(group, 128).astype(BF16), (((1,), (1,)), ((), ())),
        preferred_element_type=F32,
    )
    second = lax.broadcasted_iota(I32, (8, group), 1) % 8 >= CAP
    labs[...] = jnp.where(rows > 0.0, rows - 1.0 + jnp.where(second, float(ROWS), 0.0), -1.0)

    def dense(s):
        whole(rb.at[s], rsem.at[s])
        values = rb[s].reshape(group, 128)
        high = values.astype(BF16)
        low = (values - high.astype(F32)).astype(BF16)
        where = lax.broadcasted_iota(I32, (2 * ROWS, group), 0).astype(F32)
        spread = jnp.where(labs[pl.ds(s, 1), :] == where, 1.0, 0.0).astype(BF16)
        both = jnp.dot(spread, jnp.concatenate([high, low], axis=1), preferred_element_type=F32)
        dp[s] = both[:, :128] + both[:, 128:]

    piece = ROWS // SUB
    forward, back = column(above(1)), column(above(nz - 1))

    def ahead(t, j):
        part = pl.ds(j * piece, piece)
        return remote(dp.at[t, part], fw.at[t, part], zsend.at[0, t], fsem.at[t, j], forward)

    def behind(t, j, offset=ROWS):
        part = pl.ds(offset + j * piece, piece)
        land = bw.at[t, pl.ds(j * piece, piece)]
        return remote(dp.at[t, part], land, zsend.at[1, t], bsem.at[t, j], back)

    dense(0)
    for j in range(SUB // 2):
        ahead(0, j).start()
        behind(0, SUB // 2 + j, 0).start()
    dense(1)
    fw[0, ROWS // 2 :] = jnp.zeros((ROWS // 2, 128), F32)
    bw[0, : ROWS // 2] = jnp.zeros((ROWS // 2, 128), F32)

    whole(hr, hsem.at[0])

    def add_plane(k, total):
        return total + hr[k]

    total = lax.fori_loop(1, np_, add_plane, hr[0])
    hp[...] = total.reshape(classes, 8, 128)

    @pl.loop(1, nz)
    def _(k):
        z = above(k)
        remote(hp.at[z % classes], hz.at[me_z], sent.at[2], hsem.at[1], column(z)).start()

    pltpu.make_async_copy(hp.at[me_z % classes], hz.at[me_z], hsem.at[1]).start()
    family = me_z // classes * classes

    @pl.loop(1, half)
    def _(t):
        for j in range(SUB):
            part = pl.ds(j * piece, piece)
            other = pl.ds(ROWS + j * piece, piece)

            @pl.when((t > 1) | (j < SUB // 2))
            def _():
                pltpu.make_async_copy(fw.at[t - 1, part], fw.at[t - 1, part], fsem.at[t - 1, j]).wait()

            dp[t, part] += fw[t - 1, part]
            ahead(t, j).start()

            @pl.when((t > 1) | (j >= SUB // 2))
            def _():
                pltpu.make_async_copy(bw.at[t - 1, part], bw.at[t - 1, part], bsem.at[t - 1, j]).wait()

            dp[t, other] += bw[t - 1, part]
            behind(t, j).start()

        @pl.when(t == half // 2)
        def _():
            whole(hz, hsem.at[1])
            total = hz[0]
            for k in range(1, nz):
                total += hz[k]
            hq[...] = total
            for k in range(1, classes):
                z = family + lax.rem(me_z - family + k, classes)
                remote(hq, hg.at[me_z % classes], sent.at[3], hsem.at[2], column(z)).start()
            pltpu.make_async_copy(hq, hg.at[me_z % classes], hsem.at[2]).start()

        @pl.when(t == min(half // 2 + 1, half - 1))
        def _():
            whole(hg, hsem.at[2])

            @pl.loop(1, np_)
            def _(k):
                remote(hg, ho.at[me_p], sent.at[4], hsem.at[3], plane(mate(k))).start()

            pltpu.make_async_copy(hg, ho.at[me_p], hsem.at[3]).start()

        @pl.when(t + 1 < half)
        def _():
            dense(t + 1)

    last = half - 1
    for j in range(SUB):
        part = pl.ds(j * piece, piece)
        own = dp[0, pl.ds(ROWS + j * piece, piece)]
        pltpu.make_async_copy(fw.at[last, part], fw.at[last, part], fsem.at[last, j]).wait()
        pltpu.make_async_copy(bw.at[last, part], bw.at[last, part], bsem.at[last, j]).wait()
        cold_ref[part, :] = own + fw[last, part] + bw[last, part]
    whole(ho, hsem.at[3])
    hotg_ref[...] = ho[...].reshape(hotg_ref.shape)

    @pl.loop(0, half)
    def _(s):
        whole(sb.at[s, pl.ds(0, np_ - 1)], ssem.at[s])

    for d in range(2):
        whole(dp.at[0, pl.ds(0, ROWS // 2)], zsend.at[d, 0])

        @pl.loop(1, half)
        def _(t):
            whole(dp.at[t, pl.ds(0, ROWS)], zsend.at[d, t])

    whole(lt.at[pl.ds(0, np_ - 1)], sent.at[0])
    whole(hs.at[pl.ds(0, np_ - 1)], sent.at[1])
    whole(hz.at[pl.ds(0, nz - 1)], sent.at[2])
    whole(hg.at[pl.ds(0, classes - 1)], sent.at[3])
    whole(ho.at[pl.ds(0, np_ - 1)], sent.at[4])


def adagrad(weights, moments, gradient):
    updated = moments + gradient * gradient
    return (weights - 0.5 * gradient / (jnp.sqrt(updated) + 1e-06), updated)


def body(sizes, gradients, row_ids, hot_ids, embedding, moments, hot_table, hot_moments):
    ny, nzh, nx, nc, nzl = sizes
    np_, nz = ny * nx * nc, nzh * nzl
    half = nz // 2
    hot_rows = hot_ids.shape[0] // np_
    classes = hot_rows // 8
    width = gradients.shape[1]
    vmem = pl.BlockSpec(memory_space=pltpu.VMEM)
    dma = pltpu.SemaphoreType.DMA
    cold_grad, hot_grad = pl.pallas_call(
        functools.partial(kernel, sizes),
        out_shape=(
            jax.ShapeDtypeStruct((ROWS, width), F32),
            jax.ShapeDtypeStruct((hot_ids.shape[0], width), F32),
        ),
        in_specs=[vmem] * 3,
        out_specs=(vmem, vmem),
        scratch_shapes=[
            pltpu.VMEM((np_ * nz * CAP, 128), F32),
            pltpu.VMEM((half, np_, 8, 128), F32),
            pltpu.VMEM((half, np_, 8, 128), F32),
            pltpu.VMEM((np_, 8, 128), F32),
            pltpu.VMEM((np_, 8, 128), F32),
            pltpu.VMEM((8, np_ * 8), F32),
            pltpu.VMEM((half, 2 * ROWS, 128), F32),
            pltpu.VMEM((half, ROWS, 128), F32),
            pltpu.VMEM((half, ROWS, 128), F32),
            pltpu.VMEM((np_, hot_rows, 128), F32),
            pltpu.VMEM((np_, hot_rows, 128), F32),
            pltpu.VMEM((classes, 8, 128), F32),
            pltpu.VMEM((nz, 8, 128), F32),
            pltpu.VMEM((8, 128), F32),
            pltpu.VMEM((classes, 8, 128), F32),
            pltpu.VMEM((np_, classes, 8, 128), F32),
            dma((half,)),
            dma((half,)),
            dma,
            dma((2, half)),
            dma((half, SUB)),
            dma((half, SUB)),
            dma((4,)),
            dma((5,)),
        ],
        compiler_params=pltpu.CompilerParams(collective_id=0, has_side_effects=True),
    )(row_ids.reshape(-1, 128), hot_ids.reshape(-1, 128), gradients)
    new_table, new_moments = adagrad(embedding, moments, cold_grad)
    new_hot_table, new_hot_moments = adagrad(hot_table, hot_moments, hot_grad)
    return (new_table, new_moments, new_hot_table, new_hot_moments)


def program(torus):
    sizes = tuple(torus.shape[a] for a in AXES)
    rows = P(AXES, None)
    return jax.shard_map(
        functools.partial(body, sizes),
        mesh=torus,
        in_specs=(rows, P(AXES), P(), rows, rows, P(), P()),
        out_specs=(rows, rows, P(), P()),
        check_vma=False,
    )


def solution(mesh):
    shape = (mesh.shape["gx"] // 2, 2, mesh.shape["gy"] // 2, 2, mesh.shape["gz"])
    return program(Mesh(mesh.devices.reshape(shape), AXES))
```

time: 489 us -> 70.1 us (0.14)
  the two profiles are of different devices: /device:TPU:1 before, /device:TPU:8 now
where the time goes in v1:
time: 70.1 us; the launch traced here: 69.9 us
  Pallas kernels  65.9 us (94%)
  other arithmetic  3.35 us (5%)
    pallas_call x1, Pallas kernels, body(): pl.pallas_call(functools.partial(kernel, sizes), out_shape=(jax.ShapeDtyp...  65.9 us
    sub x2, other arithmetic, adagrad(): return (weights - 0.5 * gradient / (jnp.sqrt(updated) + 1e-06), updated)  3.35 us

profile of v1, /device:TPU:8, one launch (start us, length us, event | category | flops | bytes accessed | tf_op | source)
XLA Modules:
  0.0 69.9 jit_solution(11464377619500023996)
XLA Ops:
  0.6 65.9 %shard_map.102 = (f32[256,128]{1,0:T(8,128)}, f32[1024,128]{1,0:T(8,128)}) custom-call(s32[8,128]{1,0:T(8,128)} %bitcast.2, s32[8,128]{1,0:T(8,128)} %bitcast.3, bf16[1024,128]{1,0:T(8,128)(2,1)} %grad_ref.1), custom_call_target="tpu_custom_call" | custom-call | tf_op jit(solution)/shard_map/pallas_call | solution.py:298
  66.5 0.0 copy-start
  66.6 0.0 copy-start.1
  66.6 0.0 copy-start.2
  66.6 2.6 %divide_subtract_fusion = (f32[1024,128]{1,0:T(8,128)}, f32[1024,128]{1,0:T(8,128)}) fusion(f32[1024,128]{1,0:T(8,128)} %param.12, f32[1024,128]{1,0:T(8,128)} %get-tuple-element.7, f32[1024,128]{1,0:T(8,128)} %param.13), kind=kLoop, calls=%fused_computation | loop fusion | flops 786432 | bytes 2621440 | tf_op jit(solution)/shard_map/sub | solution.py:286
  69.2 0.0 copy-done
  69.2 0.0 copy-done.1
  69.2 0.0 copy-done.2
  69.2 0.8 %divide_subtract_fusion.1 = (f32[256,128]{1,0:T(8,128)}, f32[256,128]{1,0:T(8,128)}) fusion(f32[256,128]{1,0:T(8,128)S(1)} %copy-done, f32[256,128]{1,0:T(8,128)S(1)} %copy-done.2, f32[256,128]{1,0:T(8,128)S(1)} %copy-done.1), kind=kLoop, calls=%fused_computation.2 | loop fusion | flops 196608 | bytes 655360 | tf_op jit(solution)/shard_map/sub | solution.py:286
Async XLA Ops:
  66.5 2.6 %copy-start = (f32[256,128]{1,0:T(8,128)S(1)}, f32[256,128]{1,0:T(8,128)}, u32[]{:S(2)}) copy-start(f32[256,128]{1,0:T(8,128)} %param.10) | copy-start | bytes 393220
  66.6 2.6 %copy-start.1 = (f32[256,128]{1,0:T(8,128)S(1)}, f32[256,128]{1,0:T(8,128)}, u32[]{:S(2)}) copy-start(f32[256,128]{1,0:T(8,128)} %param.11) | copy-start | bytes 393220
  66.6 2.6 %copy-start.2 = (f32[256,128]{1,0:T(8,128)S(1)}, f32[256,128]{1,0:T(8,128)}, u32[]{:S(2)}) copy-start(f32[256,128]{1,0:T(8,128)} %get-tuple-element.6) | copy-start | bytes 393220

commit v2 on v1

v2 whole, which is shorter than its diff:
```python
import functools

import jax
import jax.numpy as jnp
from jax import lax
from jax.experimental import pallas as pl
from jax.experimental.pallas import tpu as pltpu
from jax.sharding import Mesh
from jax.sharding import PartitionSpec as P

AXES = ("gx_0", "gx_1", "gy_0", "gy_1", "gz")
CAP = 4
ROWS = 256
BIG = 1.0e9
SUB = 4
MESH = pl.DeviceIdType.MESH
F32, BF16, I32 = jnp.float32, jnp.bfloat16, jnp.int32


def half_of(n):
    return n.bit_length() - 1


def over(v, n):
    return v >> half_of(n)


def under(v, n):
    return v & (n - 1)


NEAR = ((8, 7), (6, 5), (-7, -6), (4, -5), (3, -4), (2, -3), (1, -2), (0, -1))
SHIFT = (3, 1, -2)
FAR = len(SHIFT)
STEPS = 5


def kernel(
    sizes, ids_ref, hot_ref, grad_ref, cold_ref, hotg_ref,
    hc, mc, sb, rb, lt, lr, labs, dp, fw, bw, hs, hr, hp, hz, hq, hg, ho,
    ssem, rsem, lsend, lsem, zsend, fsem, bsem, hsem, sent,
):
    ny, nzh, nx, nc, nzl = sizes
    np_, nz = ny * nx * nc, nzh * nzl
    tiles = ids_ref.shape[0]
    hot_rows = hs.shape[1]
    classes = hot_rows // 8
    group = np_ * 8
    y, zh, x, c, zl = (lax.axis_index(a) for a in AXES)
    me_p = (y * nx + x) * nc + c
    me_z = zh * nzl + zl
    sign = 1 - 2 * c

    def at(p, z):
        return (over(p, nx * nc), over(z, nzl), under(over(p, nc), nx), under(p, nc), under(z, nzl))

    def plane(p):
        return at(p, me_z)

    def column(z):
        return at(me_p, z)

    def mate(k):
        return under(me_p + k, np_)

    def above(k):
        return under(me_z + nz + k, nz)

    def remote(src, dst, send, recv, device):
        return pltpu.make_async_remote_copy(
            src_ref=src, dst_ref=dst, send_sem=send, recv_sem=recv,
            device_id=device, device_id_type=MESH,
        )

    def whole(ref, sem):
        pltpu.make_async_copy(ref, ref, sem).wait()

    barrier = pltpu.get_barrier_semaphore()

    def greet(device):
        pl.semaphore_signal(barrier, inc=1, device_id=device, device_id_type=MESH)

    for shift in SHIFT:

        @pl.loop(0, np_)
        def _(k):
            greet(at(mate(k), above(-sign * shift)))

    @pl.loop(1, np_)
    def _(k):
        greet(plane(mate(k)))

    @pl.loop(1, nz)
    def _(k):
        greet(column(above(k)))

    idf = [ids_ref[k : k + 1, :].astype(F32) for k in range(tiles)]
    found = [jnp.zeros((8, 128), F32) for _ in range(tiles)]
    for i in range(hot_ref.shape[0]):
        row = hot_ref[i : i + 1, :].astype(F32)
        column_of = jnp.transpose(jnp.broadcast_to(row, (128, 128)))
        hc[i * 128 : (i + 1) * 128, :] = column_of
        for r in range(16):
            part = column_of[r * 8 : r * 8 + 8]
            found = [jnp.where(part == idf[k], 1.0, found[k]) for k in range(tiles)]

    cold = [
        jnp.where(jnp.max(found[k], axis=0, keepdims=True) > 0.0, -1.0, idf[k])
        for k in range(tiles)
    ]
    pair = lax.broadcasted_iota(I32, (np_ * 2, 128), 0)
    col = over(pair, 2)
    turn = 1 - 2 * under(col, nc)
    floors = []
    for near in NEAR:
        z = under(me_z + nz + turn * jnp.where(under(pair, 2) == 0, *near), nz)
        o = (over(col, nx * nc) * nzh + over(z, nzl)) * nx + under(over(col, nc), nx)
        o = (o * nc + under(col, nc)) * nzl + under(z, nzl)
        floors.append((o * ROWS).astype(F32))
    lows = [f - 1.0 for f in floors]
    for j in range(CAP):
        for s in range(len(NEAR)):
            low = jnp.where(cold[0] > lows[s], cold[0], BIG)
            for k in range(1, tiles):
                low = jnp.minimum(low, jnp.where(cold[k] > lows[s], cold[k], BIG))
            low = jnp.broadcast_to(jnp.min(low, axis=1, keepdims=True), pair.shape)
            lows[s] = jnp.where(low < floors[s] + float(ROWS), low, BIG)
            mc[pl.ds(s * group + j, np_ * 2, stride=CAP), :] = lows[s]

    lane = lax.broadcasted_iota(I32, (group, 128), 1)
    slot = under(lax.broadcasted_iota(I32, (group, 128), 0), 8)
    total = jnp.zeros((group, 128), F32)
    for s in range(len(NEAR)):
        low = mc[s * group : (s + 1) * group, :]
        value = jnp.where(low < BIG, under(low.astype(I32), ROWS).astype(F32) + 1.0, 0.0)
        total = jnp.where(lane == s * 8 + slot, value, total)
    lt[...] = jnp.sum(total.reshape(np_, 8, 128), axis=1, keepdims=True)

    pl.semaphore_wait(barrier, FAR * np_ + np_ - 1 + nz - 1)

    def target(s, p):
        return at(p, above((1 - 2 * under(p, nc)) * SHIFT[s]))

    for s in range(FAR):

        @pl.loop(0, np_)
        def _(k):
            p = mate(k)
            remote(lt.at[p], lr.at[s, me_p], lsend.at[s], lsem.at[s], target(s, p)).start()

    @pl.loop(1, np_)
    def _(k):
        p = mate(k)
        remote(lt.at[p], lr.at[FAR, me_p], lsend.at[FAR], lsem.at[FAR], plane(p)).start()

    pltpu.make_async_copy(lt.at[me_p], lr.at[FAR, me_p], lsem.at[FAR]).start()

    grads = grad_ref[...]

    def slots(s):
        low = mc[pl.ds(pl.multiple_of(s * group, group), group), :]
        hits = [jnp.where(low == idf[k], 1.0, 0.0).astype(BF16) for k in range(tiles)]
        sums = jnp.dot(jnp.concatenate(hits, axis=1), grads, preferred_element_type=F32)
        sb[s] = sums.reshape(np_, 8, 128)

    def share(s):
        slots(s)

        @pl.loop(1, np_)
        def _(k):
            p = mate(k)
            remote(sb.at[s, p], rb.at[s, me_p], ssem.at[s], rsem.at[s], plane(p)).start()

        pltpu.make_async_copy(sb.at[s, me_p], rb.at[s, me_p], rsem.at[s]).start()

    for s in (0, 2, 1):
        slots(s)

        @pl.loop(0, np_)
        def _(k):
            p = mate(k)
            remote(sb.at[s, p], rb.at[s, me_p], ssem.at[s], rsem.at[s], target(s, p)).start()

    share(FAR)

    @pl.loop(0, hs.shape[0] * hot_rows // 128)
    def _(i):
        part = hc[pl.ds(pl.multiple_of(i * 128, 128), 128), :]
        hits = [jnp.where(part == idf[k], 1.0, 0.0).astype(BF16) for k in range(tiles)]
        sums = jnp.dot(jnp.concatenate(hits, axis=1), grads, preferred_element_type=F32)
        parts = 128 // hot_rows
        hs[pl.ds(i * parts, parts)] = sums.reshape(parts, hot_rows, 128)

    @pl.loop(1, np_)
    def _(k):
        p = mate(k)
        remote(hs.at[p], hr.at[me_p], sent.at[1], hsem.at[0], plane(p)).start()

    pltpu.make_async_copy(hs.at[me_p], hr.at[me_p], hsem.at[0]).start()

    @pl.loop(FAR + 1, len(NEAR))
    def _(s):
        share(s)

    for s in range(FAR + 1):
        whole(lr.at[s], lsem.at[s])
    lane = lax.broadcasted_iota(I32, (np_, 128), 1)
    known = lr[FAR].reshape(np_, 128)
    for s in range(FAR):
        known = jnp.where(over(lane, 8) == s, lr[s].reshape(np_, 128), known)
    spread = over(lax.broadcasted_iota(I32, (group, np_), 0), 8)
    spread = spread == lax.broadcasted_iota(I32, (group, np_), 1)
    wide = jnp.dot(
        jnp.where(spread, 1.0, 0.0).astype(BF16), known.astype(BF16), preferred_element_type=F32
    )
    lane = lax.broadcasted_iota(I32, (group, 128), 1)
    wide = jnp.where(under(lane, 8) == slot, wide, 0.0).astype(BF16)
    tile = over(lax.broadcasted_iota(I32, (8, 128), 1), 8)
    tile = tile == lax.broadcasted_iota(I32, (8, 128), 0)
    rows = lax.dot_general(
        jnp.where(tile, 1.0, 0.0).astype(BF16), wide, (((1,), (1,)), ((), ())),
        preferred_element_type=F32,
    )
    second = under(lax.broadcasted_iota(I32, (8, group), 1), 8) >= CAP
    labs[...] = jnp.where(rows > 0.0, rows - 1.0 + jnp.where(second, float(ROWS), 0.0), -1.0)

    def dense(s):
        whole(rb.at[s], rsem.at[s])
        values = rb[s].reshape(group, 128)
        high = values.astype(BF16)
        low = (values - high.astype(F32)).astype(BF16)
        where = lax.broadcasted_iota(I32, (2 * ROWS, group), 0).astype(F32)
        spread = jnp.where(labs[pl.ds(s, 1), :] == where, 1.0, 0.0).astype(BF16)
        both = jnp.dot(spread, jnp.concatenate([high, low], axis=1), preferred_element_type=F32)
        both = both[:, :128] + both[:, 128:]
        return both[:ROWS], both[ROWS:]

    piece = ROWS // SUB
    front, rear = column(above(sign)), column(above(-sign))
    main, side = pl.ds(0, ROWS), pl.ds(ROWS, ROWS)

    def send(i, j):
        part = pl.ds(j * piece, piece)
        other = pl.ds(ROWS + j * piece, piece)
        return (
            remote(dp.at[i, part], fw.at[i, part], zsend.at[0, i], fsem.at[i, j], front),
            remote(dp.at[i, other], bw.at[i, part], zsend.at[1, i], bsem.at[i, j], rear),
        )

    dp[0, main], dp[1, main] = dense(0)
    dp[0, side], dp[1, side] = dense(2)
    first, second = dense(1)
    dp[0, main] += first
    dp[1, main] += second
    first, second = dense(3)
    dp[1, main] += first
    dp[0, side] += second
    for j in range(SUB):
        for copy in send(0, j):
            copy.start()
    for i in range(2, STEPS):
        dp[i, side] = jnp.zeros((ROWS, 128), F32)
    dp[2, main], second = dense(4)
    dp[1, side] += second

    whole(hr, hsem.at[0])

    def add_plane(k, total):
        return total + hr[k]

    total = lax.fori_loop(1, np_, add_plane, hr[0])
    hp[...] = total.reshape(classes, 8, 128)

    @pl.loop(1, nz)
    def _(k):
        z = above(k)
        remote(hp.at[under(z, classes)], hz.at[me_z], sent.at[2], hsem.at[1], column(z)).start()

    pltpu.make_async_copy(hp.at[under(me_z, classes)], hz.at[me_z], hsem.at[1]).start()
    family = me_z - under(me_z, classes)

    @pl.loop(1, STEPS)
    def _(i):
        for j in range(SUB):
            part = pl.ds(j * piece, piece)
            other = pl.ds(ROWS + j * piece, piece)
            ahead, behind = send(i, j)
            whole(fw.at[i - 1, part], fsem.at[i - 1, j])
            dp[i, part] += fw[i - 1, part]
            ahead.start()
            whole(bw.at[i - 1, part], bsem.at[i - 1, j])
            dp[i, other] += bw[i - 1, part]
            behind.start()

        @pl.when(i == 2)
        def _():
            whole(hz, hsem.at[1])
            total = hz[0]
            for k in range(1, nz):
                total += hz[k]
            hq[...] = total
            for k in range(1, classes):
                z = family + under(me_z + k, classes)
                here = hg.at[under(me_z, classes)]
                remote(hq, here, sent.at[3], hsem.at[2], column(z)).start()
            pltpu.make_async_copy(hq, hg.at[under(me_z, classes)], hsem.at[2]).start()

        @pl.when(i == 3)
        def _():
            whole(hg, hsem.at[2])

            @pl.loop(1, np_)
            def _(k):
                remote(hg, ho.at[me_p], sent.at[4], hsem.at[3], plane(mate(k))).start()

            pltpu.make_async_copy(hg, ho.at[me_p], hsem.at[3]).start()

        @pl.when(i + 4 < len(NEAR))
        def _():
            first, second = dense(i + 4)
            dp[i + 2, main] = first
            dp[i + 1, side] += second

    last = STEPS - 1
    for j in range(SUB):
        part = pl.ds(j * piece, piece)
        whole(fw.at[last, part], fsem.at[last, j])
        whole(bw.at[last, part], bsem.at[last, j])
        cold_ref[part, :] = dp[STEPS, part] + fw[last, part] + bw[last, part]
    whole(ho, hsem.at[3])
    hotg_ref[...] = ho[...].reshape(hotg_ref.shape)

    for s in range(FAR):
        whole(sb.at[s], ssem.at[s])
        whole(lt, lsend.at[s])
    whole(lt.at[pl.ds(0, np_ - 1)], lsend.at[FAR])

    @pl.loop(FAR, len(NEAR))
    def _(s):
        whole(sb.at[s, pl.ds(0, np_ - 1)], ssem.at[s])

    @pl.loop(0, STEPS)
    def _(i):
        whole(fw.at[i], zsend.at[0, i])
        whole(bw.at[i], zsend.at[1, i])

    whole(hs.at[pl.ds(0, np_ - 1)], sent.at[1])
    whole(hz.at[pl.ds(0, nz - 1)], sent.at[2])
    whole(hg.at[pl.ds(0, classes - 1)], sent.at[3])
    whole(ho.at[pl.ds(0, np_ - 1)], sent.at[4])


def adagrad(weights, moments, gradient):
    updated = moments + gradient * gradient
    return (weights - 0.5 * gradient / (jnp.sqrt(updated) + 1e-06), updated)


def body(sizes, gradients, row_ids, hot_ids, embedding, moments, hot_table, hot_moments):
    ny, nzh, nx, nc, nzl = sizes
    np_, nz = ny * nx * nc, nzh * nzl
    tiles = len(NEAR)
    hot_rows = hot_ids.shape[0] // np_
    classes = hot_rows // 8
    width = gradients.shape[1]
    vmem = pl.BlockSpec(memory_space=pltpu.VMEM)
    dma = pltpu.SemaphoreType.DMA
    cold_grad, hot_grad = pl.pallas_call(
        functools.partial(kernel, sizes),
        out_shape=(
            jax.ShapeDtypeStruct((ROWS, width), F32),
            jax.ShapeDtypeStruct((hot_ids.shape[0], width), F32),
        ),
        in_specs=[vmem] * 3,
        out_specs=(vmem, vmem),
        scratch_shapes=[
            pltpu.VMEM((hot_ids.shape[0], 128), F32),
            pltpu.VMEM((tiles * np_ * 8, 128), F32),
            pltpu.VMEM((tiles, np_, 8, 128), F32),
            pltpu.VMEM((tiles, np_, 8, 128), F32),
            pltpu.VMEM((np_, 1, 128), F32),
            pltpu.VMEM((FAR + 1, np_, 1, 128), F32),
            pltpu.VMEM((8, np_ * 8), F32),
            pltpu.VMEM((STEPS + 1, 2 * ROWS, 128), F32),
            pltpu.VMEM((STEPS, ROWS, 128), F32),
            pltpu.VMEM((STEPS, ROWS, 128), F32),
            pltpu.VMEM((np_, hot_rows, 128), F32),
            pltpu.VMEM((np_, hot_rows, 128), F32),
            pltpu.VMEM((classes, 8, 128), F32),
            pltpu.VMEM((nz, 8, 128), F32),
            pltpu.VMEM((8, 128), F32),
            pltpu.VMEM((classes, 8, 128), F32),
            pltpu.VMEM((np_, classes, 8, 128), F32),
            dma((tiles,)),
            dma((tiles,)),
            dma((FAR + 1,)),
            dma((FAR + 1,)),
            dma((2, STEPS)),
            dma((STEPS, SUB)),
            dma((STEPS, SUB)),
            dma((4,)),
            dma((5,)),
        ],
        compiler_params=pltpu.CompilerParams(collective_id=0, has_side_effects=True),
    )(row_ids.reshape(-1, 128), hot_ids.reshape(-1, 128), gradients)
    new_table, new_moments = adagrad(embedding, moments, cold_grad)
    new_hot_table, new_hot_moments = adagrad(hot_table, hot_moments, hot_grad)
    return (new_table, new_moments, new_hot_table, new_hot_moments)


def program(torus):
    sizes = tuple(torus.shape[a] for a in AXES)
    rows = P(AXES, None)
    return jax.shard_map(
        functools.partial(body, sizes),
        mesh=torus,
        in_specs=(rows, P(AXES), P(), rows, rows, P(), P()),
        out_specs=(rows, rows, P(), P()),
        check_vma=False,
    )


def solution(mesh):
    shape = (mesh.shape["gx"] // 2, 2, mesh.shape["gy"] // 2, 2, mesh.shape["gz"])
    return program(Mesh(mesh.devices.reshape(shape), AXES))
```

time: 70.1 us -> 67.7 us (0.966)
  the two profiles are of different devices: /device:TPU:8 before, /device:TPU:1 now
where the time goes in v2:
time: 67.7 us; the launch traced here: 67.6 us
  Pallas kernels  63.5 us (94%)
  other arithmetic  3.35 us (5%)
    pallas_call x1, Pallas kernels, body(): pl.pallas_call(functools.partial(kernel, sizes), out_shape=(jax.ShapeDtyp...  63.5 us
    sub x2, other arithmetic, adagrad(): return (weights - 0.5 * gradient / (jnp.sqrt(updated) + 1e-06), updated)  3.35 us

profile of v2, /device:TPU:1, one launch (start us, length us, event | category | flops | bytes accessed | tf_op | source)
XLA Modules:
  0.0 67.6 jit_solution(16748980556815955559)
XLA Ops:
  0.6 63.5 %shard_map.102 = (f32[256,128]{1,0:T(8,128)}, f32[1024,128]{1,0:T(8,128)}) custom-call(s32[8,128]{1,0:T(8,128)} %bitcast.2, s32[8,128]{1,0:T(8,128)} %bitcast.3, bf16[1024,128]{1,0:T(8,128)(2,1)} %grad_ref.1), custom_call_target="tpu_custom_call" | custom-call | tf_op jit(solution)/shard_map/pallas_call | solution.py:367
  64.2 0.0 copy-start
  64.2 0.0 copy-start.1
  64.2 0.0 copy-start.2
  64.2 2.6 %divide_subtract_fusion = (f32[1024,128]{1,0:T(8,128)}, f32[1024,128]{1,0:T(8,128)}) fusion(f32[1024,128]{1,0:T(8,128)} %param.12, f32[1024,128]{1,0:T(8,128)} %get-tuple-element.7, f32[1024,128]{1,0:T(8,128)} %param.13), kind=kLoop, calls=%fused_computation | loop fusion | flops 786432 | bytes 2621440 | tf_op jit(solution)/shard_map/sub | solution.py:355
  66.8 0.0 copy-done
  66.8 0.0 copy-done.1
  66.8 0.0 copy-done.2
  66.8 0.8 %divide_subtract_fusion.1 = (f32[256,128]{1,0:T(8,128)}, f32[256,128]{1,0:T(8,128)}) fusion(f32[256,128]{1,0:T(8,128)S(1)} %copy-done, f32[256,128]{1,0:T(8,128)S(1)} %copy-done.2, f32[256,128]{1,0:T(8,128)S(1)} %copy-done.1), kind=kLoop, calls=%fused_computation.2 | loop fusion | flops 196608 | bytes 655360 | tf_op jit(solution)/shard_map/sub | solution.py:355
Async XLA Ops:
  64.2 2.6 %copy-start = (f32[256,128]{1,0:T(8,128)S(1)}, f32[256,128]{1,0:T(8,128)}, u32[]{:S(2)}) copy-start(f32[256,128]{1,0:T(8,128)} %param.10) | copy-start | bytes 393220
  64.2 2.6 %copy-start.1 = (f32[256,128]{1,0:T(8,128)S(1)}, f32[256,128]{1,0:T(8,128)}, u32[]{:S(2)}) copy-start(f32[256,128]{1,0:T(8,128)} %param.11) | copy-start | bytes 393220
  64.2 2.6 %copy-start.2 = (f32[256,128]{1,0:T(8,128)S(1)}, f32[256,128]{1,0:T(8,128)}, u32[]{:S(2)}) copy-start(f32[256,128]{1,0:T(8,128)} %get-tuple-element.6) | copy-start | bytes 393220

commit v3 on v2

--- a/solution.py
+++ b/solution.py
@@ -29,16 +29,17 @@
     return v & (n - 1)
 
 
-NEAR = ((8, 7), (6, 5), (-7, -6), (4, -5), (3, -4), (2, -3), (1, -2), (0, -1))
-SHIFT = (3, 1, -2)
+NEAR = ((8, 7), (6, -7), (5, -6), (4, -5), (3, -4), (2, -3), (1, -2), (0, -1))
+SHIFT = (1,)
 FAR = len(SHIFT)
-STEPS = 5
+STEPS = 7
+HOT_IN, HOT_SUM, HOT_OUT = 1, 3, 5
 
 
 def kernel(
     sizes, ids_ref, hot_ref, grad_ref, cold_ref, hotg_ref,
     hc, mc, sb, rb, lt, lr, labs, dp, fw, bw, hs, hr, hp, hz, hq, hg, ho,
-    ssem, rsem, lsend, lsem, zsend, fsem, bsem, hsem, sent,
+    ssem, rsem, lsend, lsem, zsend, fsem, bsem, hsem, sent, relay,
 ):
     ny, nzh, nx, nc, nzl = sizes
     np_, nz = ny * nx * nc, nzh * nzl
@@ -77,22 +78,19 @@
 
     barrier = pltpu.get_barrier_semaphore()
 
-    def greet(device):
-        pl.semaphore_signal(barrier, inc=1, device_id=device, device_id_type=MESH)
-
-    for shift in SHIFT:
-
-        @pl.loop(0, np_)
-        def _(k):
-            greet(at(mate(k), above(-sign * shift)))
+    def greet(sem, device):
+        pl.semaphore_signal(sem, inc=1, device_id=device, device_id_type=MESH)
+
+    greet(barrier, column(above(1)))
+    greet(barrier, column(above(-1)))
 
     @pl.loop(1, np_)
     def _(k):
-        greet(plane(mate(k)))
-
-    @pl.loop(1, nz)
-    def _(k):
-        greet(column(above(k)))
+        greet(barrier, plane(mate(k)))
+
+    def pass_on(r):
+        greet(relay.at[r], column(above(2**r)))
+        greet(relay.at[r], column(above(-(2**r))))
 
     idf = [ids_ref[k : k + 1, :].astype(F32) for k in range(tiles)]
     found = [jnp.zeros((8, 128), F32) for _ in range(tiles)]
@@ -136,25 +134,6 @@
         total = jnp.where(lane == s * 8 + slot, value, total)
     lt[...] = jnp.sum(total.reshape(np_, 8, 128), axis=1, keepdims=True)
 
-    pl.semaphore_wait(barrier, FAR * np_ + np_ - 1 + nz - 1)
-
-    def target(s, p):
-        return at(p, above((1 - 2 * under(p, nc)) * SHIFT[s]))
-
-    for s in range(FAR):
-
-        @pl.loop(0, np_)
-        def _(k):
-            p = mate(k)
-            remote(lt.at[p], lr.at[s, me_p], lsend.at[s], lsem.at[s], target(s, p)).start()
-
-    @pl.loop(1, np_)
-    def _(k):
-        p = mate(k)
-        remote(lt.at[p], lr.at[FAR, me_p], lsend.at[FAR], lsem.at[FAR], plane(p)).start()
-
-    pltpu.make_async_copy(lt.at[me_p], lr.at[FAR, me_p], lsem.at[FAR]).start()
-
     grads = grad_ref[...]
 
     def slots(s):
@@ -163,25 +142,8 @@
         sums = jnp.dot(jnp.concatenate(hits, axis=1), grads, preferred_element_type=F32)
         sb[s] = sums.reshape(np_, 8, 128)
 
-    def share(s):
+    for s in range(FAR + 1):
         slots(s)
-
-        @pl.loop(1, np_)
-        def _(k):
-            p = mate(k)
-            remote(sb.at[s, p], rb.at[s, me_p], ssem.at[s], rsem.at[s], plane(p)).start()
-
-        pltpu.make_async_copy(sb.at[s, me_p], rb.at[s, me_p], rsem.at[s]).start()
-
-    for s in (0, 2, 1):
-        slots(s)
-
-        @pl.loop(0, np_)
-        def _(k):
-            p = mate(k)
-            remote(sb.at[s, p], rb.at[s, me_p], ssem.at[s], rsem.at[s], target(s, p)).start()
-
-    share(FAR)
 
     @pl.loop(0, hs.shape[0] * hot_rows // 128)
     def _(i):
@@ -191,16 +153,44 @@
         parts = 128 // hot_rows
         hs[pl.ds(i * parts, parts)] = sums.reshape(parts, hot_rows, 128)
 
-    @pl.loop(1, np_)
-    def _(k):
-        p = mate(k)
-        remote(hs.at[p], hr.at[me_p], sent.at[1], hsem.at[0], plane(p)).start()
-
-    pltpu.make_async_copy(hs.at[me_p], hr.at[me_p], hsem.at[0]).start()
-
-    @pl.loop(FAR + 1, len(NEAR))
+    pl.semaphore_wait(barrier, 2 + np_ - 1)
+    pass_on(0)
+
+    def share(src, dst, send, recv):
+        @pl.loop(1, np_)
+        def _(k):
+            p = mate(k)
+            remote(src.at[p], dst.at[me_p], send, recv, plane(p)).start()
+
+        pltpu.make_async_copy(src.at[me_p], dst.at[me_p], recv).start()
+
+    def share_far(src, dst, send, recv, shift):
+        @pl.loop(0, np_)
+        def _(k):
+            p = mate(k)
+            z = above((1 - 2 * under(p, nc)) * shift)
+            remote(src.at[p], dst.at[me_p], send, recv, at(p, z)).start()
+
+    share(lt, lr.at[FAR], lsend.at[FAR], lsem.at[FAR])
+    share(sb.at[FAR], rb.at[FAR], ssem.at[FAR], rsem.at[FAR])
+    pl.semaphore_wait(relay.at[0], 2)
+    pass_on(1)
+    for s in range(FAR):
+        share_far(lt, lr.at[s], lsend.at[s], lsem.at[s], SHIFT[s])
+        share_far(sb.at[s], rb.at[s], ssem.at[s], rsem.at[s], SHIFT[s])
+
+    def near(s):
+        slots(s)
+        share(sb.at[s], rb.at[s], ssem.at[s], rsem.at[s])
+
+    near(FAR + 1)
+    share(hs, hr, sent.at[1], hsem.at[0])
+    pl.semaphore_wait(relay.at[1], 2)
+    pass_on(2)
+
+    @pl.loop(FAR + 2, len(NEAR))
     def _(s):
-        share(s)
+        near(s)
 
     for s in range(FAR + 1):
         whole(lr.at[s], lsem.at[s])
@@ -248,35 +238,14 @@
         )
 
     dp[0, main], dp[1, main] = dense(0)
-    dp[0, side], dp[1, side] = dense(2)
     first, second = dense(1)
-    dp[0, main] += first
-    dp[1, main] += second
-    first, second = dense(3)
     dp[1, main] += first
-    dp[0, side] += second
+    dp[0, side] = second
     for j in range(SUB):
         for copy in send(0, j):
             copy.start()
-    for i in range(2, STEPS):
-        dp[i, side] = jnp.zeros((ROWS, 128), F32)
-    dp[2, main], second = dense(4)
-    dp[1, side] += second
-
-    whole(hr, hsem.at[0])
-
-    def add_plane(k, total):
-        return total + hr[k]
-
-    total = lax.fori_loop(1, np_, add_plane, hr[0])
-    hp[...] = total.reshape(classes, 8, 128)
-
-    @pl.loop(1, nz)
-    def _(k):
-        z = above(k)
-        remote(hp.at[under(z, classes)], hz.at[me_z], sent.at[2], hsem.at[1], column(z)).start()
-
-    pltpu.make_async_copy(hp.at[under(me_z, classes)], hz.at[me_z], hsem.at[1]).start()
+    dp[2, main], dp[1, side] = dense(2)
+
     family = me_z - under(me_z, classes)
 
     @pl.loop(1, STEPS)
@@ -292,7 +261,26 @@
             dp[i, other] += bw[i - 1, part]
             behind.start()
 
-        @pl.when(i == 2)
+        @pl.when(i == HOT_IN)
+        def _():
+            whole(hr, hsem.at[0])
+
+            def add_plane(k, total):
+                return total + hr[k]
+
+            total = lax.fori_loop(1, np_, add_plane, hr[0])
+            hp[...] = total.reshape(classes, 8, 128)
+
+            pl.semaphore_wait(relay.at[2], 2)
+
+            @pl.loop(1, nz)
+            def _(k):
+                z = above(k)
+                remote(hp.at[under(z, classes)], hz.at[me_z], sent.at[2], hsem.at[1], column(z)).start()
+
+            pltpu.make_async_copy(hp.at[under(me_z, classes)], hz.at[me_z], hsem.at[1]).start()
+
+        @pl.when(i == HOT_SUM)
         def _():
             whole(hz, hsem.at[1])
             total = hz[0]
@@ -305,7 +293,7 @@
                 remote(hq, here, sent.at[3], hsem.at[2], column(z)).start()
             pltpu.make_async_copy(hq, hg.at[under(me_z, classes)], hsem.at[2]).start()
 
-        @pl.when(i == 3)
+        @pl.when(i == HOT_OUT)
         def _():
             whole(hg, hsem.at[2])
 
@@ -315,11 +303,9 @@
 
             pltpu.make_async_copy(hg, ho.at[me_p], hsem.at[3]).start()
 
-        @pl.when(i + 4 < len(NEAR))
+        @pl.when(i + 2 < len(NEAR))
         def _():
-            first, second = dense(i + 4)
-            dp[i + 2, main] = first
-            dp[i + 1, side] += second
+            dp[i + 2, main], dp[i + 1, side] = dense(i + 2)
 
     last = STEPS - 1
     for j in range(SUB):
@@ -399,6 +385,7 @@
             dma((STEPS, SUB)),
             dma((4,)),
             dma((5,)),
+            pltpu.SemaphoreType.REGULAR((3,)),
         ],
         compiler_params=pltpu.CompilerParams(collective_id=0, has_side_effects=True),
     )(row_ids.reshape(-1, 128), hot_ids.reshape(-1, 128), gradients)

time: 67.7 us -> 59.7 us (0.88)
  Pallas kernels: 63.5 us -> 55.5 us
    pallas_call x1, Pallas kernels: 63.5 us -> 55.5 us  [body(): pl.pallas_call(functools.partial(kernel, sizes), out_shape=(jax.ShapeDtyp...]
where the time goes in v3:
time: 59.7 us; the launch traced here: 59.5 us
  Pallas kernels  55.5 us (93%)
  other arithmetic  3.35 us (6%)
  between operations  0.67 us (1%)
    pallas_call x1, Pallas kernels, body(): pl.pallas_call(functools.partial(kernel, sizes), out_shape=(jax.ShapeDtyp...  55.5 us
    sub x2, other arithmetic, adagrad(): return (weights - 0.5 * gradient / (jnp.sqrt(updated) + 1e-06), updated)  3.35 us

profile of v3, /device:TPU:1, one launch (start us, length us, event | category | flops | bytes accessed | tf_op | source)
XLA Modules:
  0.0 59.5 jit_solution(2015422690886895253)
XLA Ops:
  0.6 55.5 %shard_map.102 = (f32[256,128]{1,0:T(8,128)}, f32[1024,128]{1,0:T(8,128)}) custom-call(s32[8,128]{1,0:T(8,128)} %bitcast.2, s32[8,128]{1,0:T(8,128)} %bitcast.3, bf16[1024,128]{1,0:T(8,128)(2,1)} %grad_ref.1), custom_call_target="tpu_custom_call" | custom-call | tf_op jit(solution)/shard_map/pallas_call | solution.py:353
  56.1 0.0 copy-start
  56.1 0.0 copy-start.1
  56.1 0.0 copy-start.2
  56.1 2.6 %divide_subtract_fusion = (f32[1024,128]{1,0:T(8,128)}, f32[1024,128]{1,0:T(8,128)}) fusion(f32[1024,128]{1,0:T(8,128)} %param.12, f32[1024,128]{1,0:T(8,128)} %get-tuple-element.7, f32[1024,128]{1,0:T(8,128)} %param.13), kind=kLoop, calls=%fused_computation | loop fusion | flops 786432 | bytes 2621440 | tf_op jit(solution)/shard_map/sub | solution.py:341
  58.7 0.0 copy-done
  58.7 0.0 copy-done.1
  58.7 0.0 copy-done.2
  58.7 0.8 %divide_subtract_fusion.1 = (f32[256,128]{1,0:T(8,128)}, f32[256,128]{1,0:T(8,128)}) fusion(f32[256,128]{1,0:T(8,128)S(1)} %copy-done, f32[256,128]{1,0:T(8,128)S(1)} %copy-done.2, f32[256,128]{1,0:T(8,128)S(1)} %copy-done.1), kind=kLoop, calls=%fused_computation.2 | loop fusion | flops 196608 | bytes 655360 | tf_op jit(solution)/shard_map/sub | solution.py:341
Async XLA Ops:
  56.1 2.6 %copy-start = (f32[256,128]{1,0:T(8,128)S(1)}, f32[256,128]{1,0:T(8,128)}, u32[]{:S(2)}) copy-start(f32[256,128]{1,0:T(8,128)} %param.10) | copy-start | bytes 393220
  56.1 2.6 %copy-start.1 = (f32[256,128]{1,0:T(8,128)S(1)}, f32[256,128]{1,0:T(8,128)}, u32[]{:S(2)}) copy-start(f32[256,128]{1,0:T(8,128)} %param.11) | copy-start | bytes 393220
  56.1 2.6 %copy-start.2 = (f32[256,128]{1,0:T(8,128)S(1)}, f32[256,128]{1,0:T(8,128)}, u32[]{:S(2)}) copy-start(f32[256,128]{1,0:T(8,128)} %get-tuple-element.6) | copy-start | bytes 393220

commit v4 on v3

--- a/solution.py
+++ b/solution.py
@@ -33,7 +33,7 @@
 SHIFT = (1,)
 FAR = len(SHIFT)
 STEPS = 7
-HOT_IN, HOT_SUM, HOT_OUT = 1, 3, 5
+HOT_IN, HOT_SUM, HOT_OUT = 1, 3, 4
 
 
 def kernel(

time: 59.7 us -> 57.9 us (0.970)
  Pallas kernels: 55.5 us -> 53.4 us
    pallas_call x1, Pallas kernels: 55.5 us -> 53.4 us  [body(): pl.pallas_call(functools.partial(kernel, sizes), out_shape=(jax.ShapeDtyp...]
where the time goes in v4:
time: 57.9 us; the launch traced here: 57.4 us
  Pallas kernels  53.4 us (92%)
  other arithmetic  3.35 us (6%)
  between operations  0.67 us (1%)
    pallas_call x1, Pallas kernels, body(): pl.pallas_call(functools.partial(kernel, sizes), out_shape=(jax.ShapeDtyp...  53.4 us
    sub x2, other arithmetic, adagrad(): return (weights - 0.5 * gradient / (jnp.sqrt(updated) + 1e-06), updated)  3.35 us

profile of v4, /device:TPU:1, one launch (start us, length us, event | category | flops | bytes accessed | tf_op | source)
XLA Modules:
  0.0 57.4 jit_solution(17967052750630400462)
XLA Ops:
  0.6 53.4 %shard_map.102 = (f32[256,128]{1,0:T(8,128)}, f32[1024,128]{1,0:T(8,128)}) custom-call(s32[8,128]{1,0:T(8,128)} %bitcast.2, s32[8,128]{1,0:T(8,128)} %bitcast.3, bf16[1024,128]{1,0:T(8,128)(2,1)} %grad_ref.1), custom_call_target="tpu_custom_call" | custom-call | tf_op jit(solution)/shard_map/pallas_call | solution.py:353
  54.1 0.0 copy-start
  54.1 0.0 copy-start.1
  54.1 0.0 copy-start.2
  54.1 2.6 %divide_subtract_fusion = (f32[1024,128]{1,0:T(8,128)}, f32[1024,128]{1,0:T(8,128)}) fusion(f32[1024,128]{1,0:T(8,128)} %param.12, f32[1024,128]{1,0:T(8,128)} %get-tuple-element.7, f32[1024,128]{1,0:T(8,128)} %param.13), kind=kLoop, calls=%fused_computation | loop fusion | flops 786432 | bytes 2621440 | tf_op jit(solution)/shard_map/sub | solution.py:341
  56.7 0.0 copy-done
  56.7 0.0 copy-done.1
  56.7 0.0 copy-done.2
  56.7 0.8 %divide_subtract_fusion.1 = (f32[256,128]{1,0:T(8,128)}, f32[256,128]{1,0:T(8,128)}) fusion(f32[256,128]{1,0:T(8,128)S(1)} %copy-done, f32[256,128]{1,0:T(8,128)S(1)} %copy-done.2, f32[256,128]{1,0:T(8,128)S(1)} %copy-done.1), kind=kLoop, calls=%fused_computation.2 | loop fusion | flops 196608 | bytes 655360 | tf_op jit(solution)/shard_map/sub | solution.py:341
Async XLA Ops:
  54.1 2.6 %copy-start = (f32[256,128]{1,0:T(8,128)S(1)}, f32[256,128]{1,0:T(8,128)}, u32[]{:S(2)}) copy-start(f32[256,128]{1,0:T(8,128)} %param.10) | copy-start | bytes 393220
  54.1 2.6 %copy-start.1 = (f32[256,128]{1,0:T(8,128)S(1)}, f32[256,128]{1,0:T(8,128)}, u32[]{:S(2)}) copy-start(f32[256,128]{1,0:T(8,128)} %param.11) | copy-start | bytes 393220
  54.1 2.6 %copy-start.2 = (f32[256,128]{1,0:T(8,128)S(1)}, f32[256,128]{1,0:T(8,128)}, u32[]{:S(2)}) copy-start(f32[256,128]{1,0:T(8,128)} %get-tuple-element.6) | copy-start | bytes 393220

commit v5 on v4

--- a/solution.py
+++ b/solution.py
@@ -188,9 +188,7 @@
     pl.semaphore_wait(relay.at[1], 2)
     pass_on(2)
 
-    @pl.loop(FAR + 2, len(NEAR))
-    def _(s):
-        near(s)
+    near(FAR + 2)
 
     for s in range(FAR + 1):
         whole(lr.at[s], lsem.at[s])
@@ -244,6 +242,7 @@
     for j in range(SUB):
         for copy in send(0, j):
             copy.start()
+    near(FAR + 3)
     dp[2, main], dp[1, side] = dense(2)
 
     family = me_z - under(me_z, classes)
@@ -261,6 +260,14 @@
             dp[i, other] += bw[i - 1, part]
             behind.start()
 
+        @pl.when(i + FAR + 3 < len(NEAR))
+        def _():
+            near(i + FAR + 3)
+
+        @pl.when(i + 2 < len(NEAR))
+        def _():
+            dp[i + 2, main], dp[i + 1, side] = dense(i + 2)
+
         @pl.when(i == HOT_IN)
         def _():
             whole(hr, hsem.at[0])
@@ -302,10 +309,6 @@
                 remote(hg, ho.at[me_p], sent.at[4], hsem.at[3], plane(mate(k))).start()
 
             pltpu.make_async_copy(hg, ho.at[me_p], hsem.at[3]).start()
-
-        @pl.when(i + 2 < len(NEAR))
-        def _():
-            dp[i + 2, main], dp[i + 1, side] = dense(i + 2)
 
     last = STEPS - 1
     for j in range(SUB):

time: 57.9 us -> 59.6 us (1.029)
  Pallas kernels: 53.4 us -> 55 us
    pallas_call x1, Pallas kernels: 53.4 us -> 55 us  [body(): pl.pallas_call(functools.partial(kernel, sizes), out_shape=(jax.ShapeDtyp...]
where the time goes in v5:
time: 59.6 us; the launch traced here: 59 us
  Pallas kernels  55 us (92%)
  other arithmetic  3.35 us (6%)
  between operations  0.67 us (1%)
    pallas_call x1, Pallas kernels, body(): pl.pallas_call(functools.partial(kernel, sizes), out_shape=(jax.ShapeDtyp...  55 us
    sub x2, other arithmetic, adagrad(): return (weights - 0.5 * gradient / (jnp.sqrt(updated) + 1e-06), updated)  3.35 us

profile of v5, /device:TPU:1, one launch (start us, length us, event | category | flops | bytes accessed | tf_op | source)
XLA Modules:
  0.0 59.0 jit_solution(6341858664716757758)
XLA Ops:
  0.6 55.0 %shard_map.102 = (f32[256,128]{1,0:T(8,128)}, f32[1024,128]{1,0:T(8,128)}) custom-call(s32[8,128]{1,0:T(8,128)} %bitcast.2, s32[8,128]{1,0:T(8,128)} %bitcast.3, bf16[1024,128]{1,0:T(8,128)(2,1)} %grad_ref.1), custom_call_target="tpu_custom_call" | custom-call | tf_op jit(solution)/shard_map/pallas_call | solution.py:356
  55.6 0.0 copy-start
  55.6 0.0 copy-start.1
  55.6 0.0 copy-start.2
  55.6 2.6 %divide_subtract_fusion = (f32[1024,128]{1,0:T(8,128)}, f32[1024,128]{1,0:T(8,128)}) fusion(f32[1024,128]{1,0:T(8,128)} %param.12, f32[1024,128]{1,0:T(8,128)} %get-tuple-element.7, f32[1024,128]{1,0:T(8,128)} %param.13), kind=kLoop, calls=%fused_computation | loop fusion | flops 786432 | bytes 2621440 | tf_op jit(solution)/shard_map/sub | solution.py:344
  58.2 0.0 copy-done
  58.3 0.0 copy-done.1
  58.3 0.0 copy-done.2
  58.3 0.8 %divide_subtract_fusion.1 = (f32[256,128]{1,0:T(8,128)}, f32[256,128]{1,0:T(8,128)}) fusion(f32[256,128]{1,0:T(8,128)S(1)} %copy-done, f32[256,128]{1,0:T(8,128)S(1)} %copy-done.2, f32[256,128]{1,0:T(8,128)S(1)} %copy-done.1), kind=kLoop, calls=%fused_computation.2 | loop fusion | flops 196608 | bytes 655360 | tf_op jit(solution)/shard_map/sub | solution.py:344
Async XLA Ops:
  55.6 2.6 %copy-start = (f32[256,128]{1,0:T(8,128)S(1)}, f32[256,128]{1,0:T(8,128)}, u32[]{:S(2)}) copy-start(f32[256,128]{1,0:T(8,128)} %param.10) | copy-start | bytes 393220
  55.6 2.6 %copy-start.1 = (f32[256,128]{1,0:T(8,128)S(1)}, f32[256,128]{1,0:T(8,128)}, u32[]{:S(2)}) copy-start(f32[256,128]{1,0:T(8,128)} %param.11) | copy-start | bytes 393220
  55.6 2.6 %copy-start.2 = (f32[256,128]{1,0:T(8,128)S(1)}, f32[256,128]{1,0:T(8,128)}, u32[]{:S(2)}) copy-start(f32[256,128]{1,0:T(8,128)} %get-tuple-element.6) | copy-start | bytes 393220
